TPU v7x, 128 devices: a whole 4x4x4 slice. The times are simulated.
128 devices in a mesh: row: 8 (over z, core), col: 16 (over x, y).
Axes of the slice: x: 4, y: 4, z: 4, core: 2. Of those that a mesh axis runs over, the one named last changes fastest.
Arguments:
- far_field: float32 [16384, 16384], P('row', 'col'), may hold values from -4 to 4, as said below
- inverses: float32 [2, 256, 256], replicated, may hold values from -0.05 to 0.06, as said below
- test_table: float32 [524288, 128], P(('row', 'col')), may hold values from -1.5 to 1.5
- trial_table: float32 [524288, 128], P(('row', 'col')), may hold values from -1.5 to 1.5
- tile_list: int32 [2048, 2], P(('row', 'col')), may hold values from 0 to 127, as said below
- tile_nodes: int32 [2048, 256], P(('row', 'col')), may hold values from 0 to 4095
- strokes: float32 [16384, 256], P('col'), may hold values from -0.046875 to 0.046875
Outputs:
- factored: float32 [16384, 16384], P('row', 'col')
- stroke_image: float32 [16384, 256], P('row')
Inputs may be any that keep to these rules, and one draw needn't show every extreme that they name: `tile_list`: tile t lies in the block rows held by the grid row of its pair owner (owners in row-major order of the device grid). At most 2 tiles of one owner fall in the block columns of one grid column, and in every grid row some grid column receives exactly 2 tiles from every owner of that row. Duplicate blocks may occur. `tile_nodes`: node indices refer to the owner's own 4096 table rows. `far_field`: entries of order one with a dominant diagonal between 2 and 4. `inverses`: each inverse has a positive diagonal and full off-diagonal entries.
All inputs are finite; a program needn't handle non-finite values.
Results may differ from a plain program's by a relative error of at most 0.0001.
Values sent between devices are 32-bit elements; how exact they have to be, the bound alone decides.
A program may use at most 128 MiB of HBM per device.

v0:
```python
import jax
import jax.numpy as jnp
from jax import lax
from jax.sharding import PartitionSpec as P


def broadcast(value, axis, source):
    kept = jnp.where(lax.axis_index(axis) == source, value, 0).astype(value.dtype)
    return lax.psum(kept, axis)


def rows_share(block):
    return broadcast(block, "row", 0)


def on_device(far_field, inverses, test_table, trial_table, tile_list, tile_nodes, strokes):
    highest = lax.Precision.HIGHEST
    col_count = lax.axis_size("col")
    row_index = lax.axis_index("row")
    col_index = lax.axis_index("col")
    rows_local, cols_local = far_field.shape
    tile = test_table.shape[1]
    width = inverses.shape[1]
    owned = tile_list.shape[0]
    capacity = 2 * ((owned + col_count - 1) // col_count)
    block_rows = rows_local // tile
    block_cols = cols_local // tile
    left = test_table[tile_nodes]
    right = trial_table[tile_nodes]
    pieces = jnp.einsum(
        "tqi,tqj->tij", left, right, precision=highest, preferred_element_type=jnp.float32
    )
    pieces = pieces.reshape(owned, tile * tile)
    target = tile_list[:, 1] // block_cols
    position = jnp.arange(owned, dtype=jnp.int32)
    earlier = (target[None, :] == target[:, None]) & (position[None, :] < position[:, None])
    slot = target * capacity + jnp.sum(earlier.astype(jnp.int32), axis=1)
    picked = jnp.arange(col_count * capacity, dtype=jnp.int32)[:, None] == slot[None, :]
    local_block = (tile_list[:, 0] - row_index * block_rows) * block_cols + tile_list[
        :, 1
    ] % block_cols
    outgoing = jnp.dot(
        picked.astype(jnp.float32), pieces, precision=highest, preferred_element_type=jnp.float32
    )
    outgoing = outgoing.reshape(col_count, capacity, tile * tile)
    labels = jnp.sum(jnp.where(picked, local_block[None, :] + 1, 0), axis=1) - 1
    labels = labels.reshape(col_count, capacity)
    arrived, spots = (
        lax.all_to_all(outgoing, "col", split_axis=0, concat_axis=0, tiled=True),
        lax.all_to_all(labels, "col", split_axis=0, concat_axis=0, tiled=True),
    )
    arrived = arrived.reshape(col_count * capacity, tile * tile)
    spots = spots.reshape(col_count * capacity)
    placing = (
        jnp.arange(block_rows * block_cols, dtype=jnp.int32)[:, None] == spots[None, :]
    ).astype(jnp.float32)
    near = jnp.dot(placing, arrived, precision=highest, preferred_element_type=jnp.float32)
    near = (
        near.reshape(block_rows, block_cols, tile, tile)
        .transpose(0, 2, 1, 3)
        .reshape(rows_local, cols_local)
    )
    matrix = far_field + near
    global_rows = row_index * rows_local + jnp.arange(rows_local, dtype=jnp.int32)
    global_cols = col_index * cols_local + jnp.arange(cols_local, dtype=jnp.int32)
    first_grid_col = col_index == 0
    for panel in range(2):
        low = panel * width
        high = low + width
        lower = jnp.dot(
            matrix[:, low:high],
            inverses[panel],
            precision=highest,
            preferred_element_type=jnp.float32,
        )
        lower = jnp.where(global_rows[:, None] >= high, lower, 0.0)
        lower_all = broadcast(lower, "col", 0)
        upper = jnp.where(global_cols[None, :] >= high, matrix[low:high, :], 0.0)
        upper_all = rows_share(upper)
        matrix = matrix - jnp.dot(
            lower_all, upper_all, precision=highest, preferred_element_type=jnp.float32
        )
        renewed = jnp.where(global_rows[:, None] >= high, lower_all, matrix[:, low:high])
        matrix = matrix.at[:, low:high].set(jnp.where(first_grid_col, renewed, matrix[:, low:high]))
    partial_image = jnp.dot(matrix, strokes, precision=highest, preferred_element_type=jnp.float32)
    image = lax.psum(partial_image, "col")
    return (matrix, image)


def solution(mesh):
    return jax.shard_map(
        on_device,
        mesh=mesh,
        in_specs=(
            P("row", "col"),
            P(),
            P(("row", "col"), None),
            P(("row", "col"), None),
            P(("row", "col"), None),
            P(("row", "col"), None),
            P("col", None),
        ),
        out_specs=(P("row", "col"), P("row", None)),
        check_vma=False,
    )
```

profile of v0, /device:TPU:0, one launch (start us, length us, event | category | flops | bytes accessed | tf_op | source)
XLA Modules:
  0.0 573.1 jit_solution(1673368568827543794)
XLA Ops:
  7.2 0.8 fusion.29
  8.0 0.8 fusion.30
  8.8 0.2 convert_reduce_fusion
  9.0 0.1 select_reduce_fusion
  9.1 0.7 sub.34
  9.8 7.1 %all-to-all-start = ((s32[16,1,2]{2,1,0:T(1,128)}), s32[16,1,2]{2,1,0:T(1,128)S(1)}, u32[]{:S(2)}, u32[]{:S(2)}) async-start(s32[16,1,2]{2,1,0:T(1,128)} %bitcast.3), calls=%async_computation | async-start | bytes 16384 | tf_op jit(solution)/shard_map/all_to_all | solution.py:50
  16.9 0.7 fusion.18
  17.7 14.2 %gather_fusion = f32[4096,128]{1,0:T(8,128)} fusion(f32[4096,128]{1,0:T(8,128)S(1)} %copy-done, s32[4096]{0:T(1024)S(1)} %broadcast_clamp_fusion), kind=kCustom, calls=%fused_computation | custom fusion | bytes 4210688 | tf_op jit(solution)/shard_map/gather | solution.py:28
  31.9 15.9 %gather_fusion.1 = f32[4096,128]{1,0:T(8,128)} fusion(f32[4096,128]{1,0:T(8,128)} %param.14, s32[4096]{0:T(1024)S(1)} %broadcast_clamp_fusion), kind=kCustom, calls=%fused_computation.1 | custom fusion | bytes 4210688 | tf_op jit(solution)/shard_map/gather | solution.py:29
  47.8 5.1 fusion.31
  52.9 1.2 reshape.237
  54.1 2.2 fusion.19
  56.3 2.9 copy.19
  59.3 7.2 %all-to-all-start.1 = ((f32[16,2,16384]{2,1,0:T(2,128)}), f32[16,2,16384]{2,1,0:T(2,128)S(1)}, u32[]{:S(2)}, u32[]{:S(2)}) async-start(f32[16,2,16384]{2,1,0:T(2,128)} %copy.19), calls=%async_computation.1 | async-start | bytes 4194304 | tf_op jit(solution)/shard_map/all_to_all | solution.py:49
  66.5 0.2 all-reduce.8.cloned.1.call-start
  66.8 0.5 broadcast.303
  67.3 0.7 reduce.19
  67.9 0.1 eq.93
  68.0 27.8 %all-to-all-done.1 = f32[16,2,16384]{2,1,0:T(2,128)S(1)} async-done(((f32[16,2,16384]{2,1,0:T(2,128)}), f32[16,2,16384]{2,1,0:T(2,128)S(1)}, u32[]{:S(2)}, u32[]{:S(2)}) %all-to-all-start.1) | async-done | bytes 2097184 | tf_op jit(solution)/shard_map/all_to_all | solution.py:49
  95.8 2.4 reshape.215
  98.2 7.3 %fusion.4 = f32[16,8,128,128]{3,1,2,0:T(8,128)} fusion(s32[32]{0:T(128)S(1)} %eq.93, s32[16,8]{1,0:T(8,128)S(1)} %multiply_add_fusion, f32[32,16384]{1,0:T(8,128)} %reshape.215), kind=kOutput, calls=%fused_computation.14 | convolution fusion | flops 805310464 | bytes 10486400 | tf_op jit(solution)/shard_map/dot_general | solution.py:57
  105.6 12.1 %bitcast_add_fusion = f32[2048,1024]{1,0:T(8,128)} fusion(f32[2048,1024]{1,0:T(8,128)} %param.11, f32[256,8,8,128]{3,2,1,0:T(8,128)} %bitcast.63), kind=kLoop, calls=%fused_computation.2 | loop fusion | flops 2097152 | bytes 25165824 | tf_op jit(solution)/shard_map/add | solution.py:63
  117.7 2.4 fusion.9
  120.1 0.0 all-reduce.8.cloned.1.call-update
  120.1 0.0 all-reduce.6.cloned.1.call-start
  120.2 4.7 fusion.1
  124.9 0.0 all-reduce.6.cloned.1.call-update
  125.0 0.3 all-reduce.12.cloned.1.call-start
  125.2 0.7 compare_reduce_fusion.1
  125.9 56.5 %all-reduce.8.cloned.1.call-done = f32[256,1024]{1,0:T(8,128)} async-done(((f32[256,1024]{1,0:T(8,128)}), f32[256,1024]{1,0:T(8,128)}) %all-reduce.8.cloned.1.call-update) | async-done | bytes 1048592 | tf_op jit(solution)/shard_map/psum | solution.py:9
  182.4 94.0 %all-reduce.6.cloned.1.call-done = f32[2048,256]{1,0:T(8,128)} async-done(((f32[2048,256]{1,0:T(8,128)}), f32[2048,256]{1,0:T(8,128)}) %all-reduce.6.cloned.1.call-update) | async-done | bytes 2097168 | tf_op jit(solution)/shard_map/psum | solution.py:9
  276.5 10.6 %convolution_subtract_fusion.1 = f32[2048,1024]{1,0:T(8,128)S(1)} fusion(f32[2048,1024]{1,0:T(8,128)} %bitcast_add_fusion, f32[2048,256]{1,0:T(8,128)} %all-reduce.6.cloned.1.call-done, f32[256,1024]{1,0:T(8,128)} %all-reduce.8.cloned.1.call-done), kind=kOutput, calls=%fused_computation.4 | convolution fusion | flops 6444548096 | bytes 19922944 | tf_op jit(solution)/shard_map/dot_general | solution.py:80
  287.0 1.2 fusion.2
  288.3 3.4 copy-done.3
  291.7 1.1 fusion.8
  292.9 0.0 all-reduce.10.cloned.1.call-start
  292.9 4.7 fusion
  297.7 0.0 all-reduce.10.cloned.1.call-update
  297.7 0.3 all-reduce.14.cloned.1.call-start
  298.0 0.6 compare_reduce_fusion
  298.6 56.8 %all-reduce.12.cloned.1.call-done = f32[256,1024]{1,0:T(8,128)} async-done(((f32[256,1024]{1,0:T(8,128)}), f32[256,1024]{1,0:T(8,128)}) %all-reduce.12.cloned.1.call-update) | async-done | bytes 1048592 | tf_op jit(solution)/shard_map/psum | solution.py:9
  355.4 93.8 %all-reduce.10.cloned.1.call-done = f32[2048,256]{1,0:T(8,128)} async-done(((f32[2048,256]{1,0:T(8,128)}), f32[2048,256]{1,0:T(8,128)}) %all-reduce.10.cloned.1.call-update) | async-done | bytes 2097168 | tf_op jit(solution)/shard_map/psum | solution.py:9
  449.3 10.6 %convolution_subtract_fusion = f32[2048,1024]{1,0:T(8,128)S(1)} fusion(f32[2048,1024]{1,0:T(8,128)} %copy-done.3, f32[2048,256]{1,0:T(8,128)} %all-reduce.10.cloned.1.call-done, f32[256,1024]{1,0:T(8,128)} %all-reduce.12.cloned.1.call-done), kind=kOutput, calls=%fused_computation.3 | convolution fusion | flops 6444548096 | bytes 19922944 | tf_op jit(solution)/shard_map/dot_general | solution.py:80
  459.9 1.4 fusion.3
  461.3 3.4 copy-done.2
  464.7 8.3 %fusion.32 = f32[2048,256]{1,0:T(8,128)} fusion(f32[2048,1024]{1,0:T(8,128)S(1)} %fusion.3, f32[1024,256]{1,0:T(8,128)S(1)} %copy-done.7), kind=kOutput, calls=%fused_computation.69 | convolution fusion | flops 6442450944 | bytes 11534336 | tf_op jit(solution)/shard_map/dot_general | solution.py:85
  473.0 90.5 %all-reduce.14.cloned.1.call-done = f32[2048,256]{1,0:T(8,128)} async-done(((f32[2048,256]{1,0:T(8,128)}), f32[2048,256]{1,0:T(8,128)}) %all-reduce.14.cloned.1.call-update) | async-done | bytes 2097168 | tf_op jit(solution)/shard_map/psum | solution.py:86
  563.5 3.0 copy.38
  (29 shorter events, 0.2 us)
Async XLA Ops:
  7.2 10.5 %copy-start = (f32[4096,128]{1,0:T(8,128)S(1)}, f32[4096,128]{1,0:T(8,128)}, u32[]{:S(2)}) copy-start(f32[4096,128]{1,0:T(8,128)} %param.13) | copy-start | bytes 6291460
  9.8 49.5 %all-to-all-start = ((s32[16,1,2]{2,1,0:T(1,128)}), s32[16,1,2]{2,1,0:T(1,128)S(1)}, u32[]{:S(2)}, u32[]{:S(2)}) async-start(s32[16,1,2]{2,1,0:T(1,128)} %bitcast.3), calls=%async_computation | async-start | bytes 16384 | tf_op jit(solution)/shard_map/all_to_all | solution.py:50
  31.9 15.9 %copy-start.6 = (f32[4096,128]{1,0:T(8,128)S(1)}, f32[4096,128]{1,0:T(8,128)}, u32[]{:S(2)}) copy-start(f32[4096,128]{1,0:T(8,128)} %gather_fusion) | copy-start | bytes 6291460
  59.3 36.5 %all-to-all-start.1 = ((f32[16,2,16384]{2,1,0:T(2,128)}), f32[16,2,16384]{2,1,0:T(2,128)S(1)}, u32[]{:S(2)}, u32[]{:S(2)}) async-start(f32[16,2,16384]{2,1,0:T(2,128)} %copy.19), calls=%async_computation.1 | async-start | bytes 4194304 | tf_op jit(solution)/shard_map/all_to_all | solution.py:49
  66.5 115.9 %all-reduce.8.cloned.1.call-start = ((), (), s32[]{:S(2)}) async-start(), calls=%async_computation.3 | async-start | bytes 2097152 | tf_op jit(solution)/shard_map/psum | solution.py:9
  117.7 2.5 copy-start.8
  120.1 156.3 %all-reduce.6.cloned.1.call-start = ((), (), s32[]{:S(2)}) async-start(), calls=%async_computation.2 | async-start | bytes 4194304 | tf_op jit(solution)/shard_map/psum | solution.py:9
  125.0 230.5 %all-reduce.12.cloned.1.call-start = ((), (), s32[]{:S(2)}) async-start(), calls=%async_computation.5 | async-start | bytes 2097152 | tf_op jit(solution)/shard_map/psum | solution.py:9
  276.5 10.6 %copy-start.4 = (f32[2048,256]{1,0:T(8,128)S(1)}, f32[2048,256]{1,0:T(8,128)}, u32[]{:S(2)}) copy-start(f32[2048,256]{1,0:T(8,128)} %all-reduce.6.cloned.1.call-done) | copy-start | bytes 6291460
  288.3 3.4 copy-start.3
  292.9 156.4 %all-reduce.10.cloned.1.call-start = ((), (), s32[]{:S(2)}) async-start(), calls=%async_computation.4 | async-start | bytes 4194304 | tf_op jit(solution)/shard_map/psum | solution.py:9
  297.7 265.8 %all-reduce.14.cloned.1.call-start = ((), (), s32[]{:S(2)}) async-start(), calls=%async_computation.6 | async-start | bytes 4194304 | tf_op jit(solution)/shard_map/psum | solution.py:86
  449.3 10.6 %copy-start.5 = (f32[2048,256]{1,0:T(8,128)S(1)}, f32[2048,256]{1,0:T(8,128)}, u32[]{:S(2)}) copy-start(f32[2048,256]{1,0:T(8,128)} %all-reduce.10.cloned.1.call-done) | copy-start | bytes 6291460
  459.9 4.8 copy-start.7
  461.2 3.4 copy-start.2
  472.9 93.6 %copy-start.1 = (f32[4096,128]{1,0:T(8,128)S(1)}, f32[4096,128]{1,0:T(8,128)}, u32[]{:S(2)}) copy-start(f32[4096,128]{1,0:T(8,128)} %param.13) | copy-start | bytes 6291460
Sparse Core Ops, SparseCore 0:
  120.3 62.1 all-reduce.7
  186.3 90.0 all-reduce.5
  293.0 62.3 all-reduce.11
  359.2 90.0 all-reduce.9
  473.1 90.3 all-reduce.13
where the time goes:
time: 574 us; the launch traced here: 573 us
  waiting for transfers between devices  420 us (73%)
  matrix products  53.5 us (9%)
  local copies, waits for them, and re-layouts  47.8 us (8%)
  other arithmetic  23 us (4%)
  starting transfers between devices  15.2 us (3%)
  between operations  14 us (2%)
    psum x4, waiting for transfers between devices, broadcast(): return lax.psum(kept, axis)  301 us
    psum x1, waiting for transfers between devices, on_device(): image = lax.psum(partial_image, 'col')  90.5 us
    all_to_all x1, waiting for transfers between devices, on_device(): lax.all_to_all(outgoing, 'col', split_axis=0, concat_axis=0, tiled=True)  27.8 us
    dot_general x2, matrix products, on_device(): jnp.dot(lower_all, upper_all, precision=highest, preferred_element_type=j...  21.1 us
    gather x1, local copies, waits for them, and re-layouts, on_device(): right = trial_table[tile_nodes]  15.9 us
    gather x1, local copies, waits for them, and re-layouts, on_device(): left = test_table[tile_nodes]  14.2 us
    add x1, other arithmetic, on_device(): matrix = far_field + near  12.1 us
  transfers between devices with their start and end apart: 7, of which 6 were waited for; matrix products, arithmetic and copies ran while one was open for 9% of the time, Pallas kernels for 0%

commit v1 on v0

--- a/solution.py
+++ b/solution.py
@@ -83,7 +83,7 @@
         renewed = jnp.where(global_rows[:, None] >= high, lower_all, matrix[:, low:high])
         matrix = matrix.at[:, low:high].set(jnp.where(first_grid_col, renewed, matrix[:, low:high]))
     partial_image = jnp.dot(matrix, strokes, precision=highest, preferred_element_type=jnp.float32)
-    image = lax.psum(partial_image, "col")
+    image = jnp.sum(lax.all_gather(partial_image, "col"), axis=0)
     return (matrix, image)
 
 

time: 574 us -> 691 us (1.20)
  waiting for transfers between devices: 420 us -> 526 us
  other arithmetic: 23 us -> 36.4 us
    all_gather x0 -> x1, waiting for transfers between devices: none -> 197 us  [on_device(): image = jnp.sum(lax.all_gather(partial_image, 'col'), axis=0)]
    psum x1 -> x0, waiting for transfers between devices: 90.5 us -> none  [on_device(): image = lax.psum(partial_image, 'col')]
    reduce_sum x0 -> x1, other arithmetic: none -> 13.5 us  [on_device(): image = jnp.sum(lax.all_gather(partial_image, 'col'), axis=0)]
  transfers between devices with their start and end apart: 7 -> 7, of which waited for: 6 -> 6; matrix products, arithmetic and copies ran while one was open for 9% -> 8% of each run, Pallas kernels for 0% -> 0%
where the time goes in v1:
time: 691 us; the launch traced here: 689 us
  waiting for transfers between devices  526 us (76%)
  matrix products  53.5 us (8%)
  local copies, waits for them, and re-layouts  44.8 us (6%)
  other arithmetic  36.4 us (5%)
  starting transfers between devices  15.2 us (2%)
  between operations  14 us (2%)
    psum x4, waiting for transfers between devices, broadcast(): return lax.psum(kept, axis)  301 us
    all_gather x1, waiting for transfers between devices, on_device(): image = jnp.sum(lax.all_gather(partial_image, 'col'), axis=0)  197 us
    all_to_all x1, waiting for transfers between devices, on_device(): lax.all_to_all(outgoing, 'col', split_axis=0, concat_axis=0, tiled=True)  27.8 us
    dot_general x2, matrix products, on_device(): jnp.dot(lower_all, upper_all, precision=highest, preferred_element_type=j...  21.1 us
    gather x1, local copies, waits for them, and re-layouts, on_device(): left = test_table[tile_nodes]  15.9 us
    gather x1, local copies, waits for them, and re-layouts, on_device(): right = trial_table[tile_nodes]  14.2 us
  transfers between devices with their start and end apart: 7, of which 6 were waited for; matrix products, arithmetic and copies ran while one was open for 8% of the time, Pallas kernels for 0%

profile of v1, /device:TPU:0, one launch (start us, length us, event | category | flops | bytes accessed | tf_op | source)
XLA Modules:
  0.0 689.5 jit_solution(9226059793749268030)
XLA Ops:
  7.2 0.8 fusion.29
  8.0 0.8 fusion.30
  8.8 0.2 convert_reduce_fusion
  9.0 0.1 select_reduce_fusion
  9.1 0.7 sub.34
  9.8 7.1 %all-to-all-start = ((s32[16,1,2]{2,1,0:T(1,128)}), s32[16,1,2]{2,1,0:T(1,128)S(1)}, u32[]{:S(2)}, u32[]{:S(2)}) async-start(s32[16,1,2]{2,1,0:T(1,128)} %bitcast.3), calls=%async_computation | async-start | bytes 16384 | tf_op jit(solution)/shard_map/all_to_all | solution.py:50
  16.9 0.7 fusion.18
  17.7 14.2 %gather_fusion.1 = f32[4096,128]{1,0:T(8,128)} fusion(f32[4096,128]{1,0:T(8,128)S(1)} %copy-done, s32[4096]{0:T(1024)S(1)} %broadcast_clamp_fusion), kind=kCustom, calls=%fused_computation.1 | custom fusion | bytes 4210688 | tf_op jit(solution)/shard_map/gather | solution.py:29
  31.9 15.9 %gather_fusion = f32[4096,128]{1,0:T(8,128)} fusion(f32[4096,128]{1,0:T(8,128)} %param.13, s32[4096]{0:T(1024)S(1)} %broadcast_clamp_fusion), kind=kCustom, calls=%fused_computation | custom fusion | bytes 4210688 | tf_op jit(solution)/shard_map/gather | solution.py:28
  47.8 5.1 fusion.31
  52.9 1.2 reshape.238
  54.1 2.2 fusion.19
  56.3 2.9 copy.19
  59.3 7.2 %all-to-all-start.1 = ((f32[16,2,16384]{2,1,0:T(2,128)}), f32[16,2,16384]{2,1,0:T(2,128)S(1)}, u32[]{:S(2)}, u32[]{:S(2)}) async-start(f32[16,2,16384]{2,1,0:T(2,128)} %copy.19), calls=%async_computation.1 | async-start | bytes 4194304 | tf_op jit(solution)/shard_map/all_to_all | solution.py:49
  66.5 0.2 all-reduce.7.cloned.1.call-start
  66.8 0.5 broadcast.303
  67.3 0.7 reduce.19
  67.9 0.1 eq.93
  68.0 27.8 %all-to-all-done.1 = f32[16,2,16384]{2,1,0:T(2,128)S(1)} async-done(((f32[16,2,16384]{2,1,0:T(2,128)}), f32[16,2,16384]{2,1,0:T(2,128)S(1)}, u32[]{:S(2)}, u32[]{:S(2)}) %all-to-all-start.1) | async-done | bytes 2097184 | tf_op jit(solution)/shard_map/all_to_all | solution.py:49
  95.8 2.4 reshape.215
  98.2 7.3 %fusion.4 = f32[16,8,128,128]{3,1,2,0:T(8,128)} fusion(s32[32]{0:T(128)S(1)} %eq.93, s32[16,8]{1,0:T(8,128)S(1)} %multiply_add_fusion, f32[32,16384]{1,0:T(8,128)} %reshape.215), kind=kOutput, calls=%fused_computation.14 | convolution fusion | flops 805310464 | bytes 10486400 | tf_op jit(solution)/shard_map/dot_general | solution.py:57
  105.6 12.1 %bitcast_add_fusion = f32[2048,1024]{1,0:T(8,128)} fusion(f32[2048,1024]{1,0:T(8,128)} %param.11, f32[256,8,8,128]{3,2,1,0:T(8,128)} %bitcast.64), kind=kLoop, calls=%fused_computation.2 | loop fusion | flops 2097152 | bytes 25165824 | tf_op jit(solution)/shard_map/add | solution.py:63
  117.7 2.4 fusion.9
  120.1 0.0 all-reduce.7.cloned.1.call-update
  120.1 0.0 all-reduce.5.cloned.1.call-start
  120.2 4.7 fusion.1
  124.9 0.0 all-reduce.5.cloned.1.call-update
  125.0 0.3 all-reduce.11.cloned.1.call-start
  125.2 0.7 compare_reduce_fusion.1
  125.9 56.5 %all-reduce.7.cloned.1.call-done = f32[256,1024]{1,0:T(8,128)} async-done(((f32[256,1024]{1,0:T(8,128)}), f32[256,1024]{1,0:T(8,128)}) %all-reduce.7.cloned.1.call-update) | async-done | bytes 1048592 | tf_op jit(solution)/shard_map/psum | solution.py:9
  182.4 94.0 %all-reduce.5.cloned.1.call-done = f32[2048,256]{1,0:T(8,128)} async-done(((f32[2048,256]{1,0:T(8,128)}), f32[2048,256]{1,0:T(8,128)}) %all-reduce.5.cloned.1.call-update) | async-done | bytes 2097168 | tf_op jit(solution)/shard_map/psum | solution.py:9
  276.5 10.6 %convolution_subtract_fusion.1 = f32[2048,1024]{1,0:T(8,128)S(1)} fusion(f32[2048,1024]{1,0:T(8,128)} %bitcast_add_fusion, f32[2048,256]{1,0:T(8,128)} %all-reduce.5.cloned.1.call-done, f32[256,1024]{1,0:T(8,128)} %all-reduce.7.cloned.1.call-done), kind=kOutput, calls=%fused_computation.4 | convolution fusion | flops 6444548096 | bytes 19922944 | tf_op jit(solution)/shard_map/dot_general | solution.py:80
  287.0 1.2 fusion.2
  288.3 3.4 copy-done.3
  291.7 1.1 fusion.8
  292.9 0.0 all-reduce.9.cloned.1.call-start
  292.9 4.7 fusion
  297.7 0.3 all-gather.3.cloned.1.call-start
  298.0 0.6 compare_reduce_fusion
  298.6 56.8 %all-reduce.11.cloned.1.call-done = f32[256,1024]{1,0:T(8,128)} async-done(((f32[256,1024]{1,0:T(8,128)}), f32[256,1024]{1,0:T(8,128)}) %all-reduce.11.cloned.1.call-update) | async-done | bytes 1048592 | tf_op jit(solution)/shard_map/psum | solution.py:9
  355.4 93.8 %all-reduce.9.cloned.1.call-done = f32[2048,256]{1,0:T(8,128)} async-done(((f32[2048,256]{1,0:T(8,128)}), f32[2048,256]{1,0:T(8,128)}) %all-reduce.9.cloned.1.call-update) | async-done | bytes 2097168 | tf_op jit(solution)/shard_map/psum | solution.py:9
  449.3 10.6 %convolution_subtract_fusion = f32[2048,1024]{1,0:T(8,128)S(1)} fusion(f32[2048,1024]{1,0:T(8,128)} %copy-done.3, f32[2048,256]{1,0:T(8,128)} %all-reduce.9.cloned.1.call-done, f32[256,1024]{1,0:T(8,128)} %all-reduce.11.cloned.1.call-done), kind=kOutput, calls=%fused_computation.3 | convolution fusion | flops 6444548096 | bytes 19922944 | tf_op jit(solution)/shard_map/dot_general | solution.py:80
  459.9 1.4 fusion.3
  461.3 3.4 copy-done.2
  464.7 8.3 %fusion.32 = f32[2048,256]{1,0:T(8,128)} fusion(f32[2048,1024]{1,0:T(8,128)S(1)} %fusion.3, f32[1024,256]{1,0:T(8,128)S(1)} %copy-done.7), kind=kOutput, calls=%fused_computation.69 | convolution fusion | flops 6442450944 | bytes 11534336 | tf_op jit(solution)/shard_map/dot_general | solution.py:85
  472.9 0.0 all-gather.3.cloned.1.call-update
  472.9 196.5 %all-gather.3.cloned.1.call-done = f32[32768,256]{1,0:T(8,128)} async-done(((f32[2048,256]{1,0:T(8,128)}), f32[32768,256]{1,0:T(8,128)}) %all-gather.3.cloned.1.call-update) | async-done | bytes 33554448 | tf_op jit(solution)/shard_map/all_gather | solution.py:86
  669.5 13.5 %reduce_sum.29 = f32[2048,256]{1,0:T(8,128)} reduce(f32[16,2048,256]{2,1,0:T(8,128)} %bitcast.65, f32[]{:T(128)} %constant.113.clone.1), dimensions={0}, to_apply=%region_8.9 | reduce | flops 7864320 | bytes 35651588 | tf_op jit(solution)/shard_map/reduce_sum | solution.py:86
  (29 shorter events, 0.2 us)
Async XLA Ops:
  7.2 10.5 %copy-start = (f32[4096,128]{1,0:T(8,128)S(1)}, f32[4096,128]{1,0:T(8,128)}, u32[]{:S(2)}) copy-start(f32[4096,128]{1,0:T(8,128)} %param.14) | copy-start | bytes 6291460
  9.8 49.5 %all-to-all-start = ((s32[16,1,2]{2,1,0:T(1,128)}), s32[16,1,2]{2,1,0:T(1,128)S(1)}, u32[]{:S(2)}, u32[]{:S(2)}) async-start(s32[16,1,2]{2,1,0:T(1,128)} %bitcast.3), calls=%async_computation | async-start | bytes 16384 | tf_op jit(solution)/shard_map/all_to_all | solution.py:50
  31.9 15.9 %copy-start.6 = (f32[4096,128]{1,0:T(8,128)S(1)}, f32[4096,128]{1,0:T(8,128)}, u32[]{:S(2)}) copy-start(f32[4096,128]{1,0:T(8,128)} %gather_fusion.1) | copy-start | bytes 6291460
  59.3 36.5 %all-to-all-start.1 = ((f32[16,2,16384]{2,1,0:T(2,128)}), f32[16,2,16384]{2,1,0:T(2,128)S(1)}, u32[]{:S(2)}, u32[]{:S(2)}) async-start(f32[16,2,16384]{2,1,0:T(2,128)} %copy.19), calls=%async_computation.1 | async-start | bytes 4194304 | tf_op jit(solution)/shard_map/all_to_all | solution.py:49
  66.5 115.9 %all-reduce.7.cloned.1.call-start = ((), (), s32[]{:S(2)}) async-start(), calls=%async_computation.3 | async-start | bytes 2097152 | tf_op jit(solution)/shard_map/psum | solution.py:9
  117.7 2.5 copy-start.8
  120.1 156.3 %all-reduce.5.cloned.1.call-start = ((), (), s32[]{:S(2)}) async-start(), calls=%async_computation.2 | async-start | bytes 4194304 | tf_op jit(solution)/shard_map/psum | solution.py:9
  125.0 230.5 %all-reduce.11.cloned.1.call-start = ((), (), s32[]{:S(2)}) async-start(), calls=%async_computation.5 | async-start | bytes 2097152 | tf_op jit(solution)/shard_map/psum | solution.py:9
  276.5 10.6 %copy-start.4 = (f32[2048,256]{1,0:T(8,128)S(1)}, f32[2048,256]{1,0:T(8,128)}, u32[]{:S(2)}) copy-start(f32[2048,256]{1,0:T(8,128)} %all-reduce.5.cloned.1.call-done) | copy-start | bytes 6291460
  288.3 3.4 copy-start.3
  292.9 156.4 %all-reduce.9.cloned.1.call-start = ((), (), s32[]{:S(2)}) async-start(), calls=%async_computation.4 | async-start | bytes 4194304 | tf_op jit(solution)/shard_map/psum | solution.py:9
  297.7 371.8 %all-gather.3.cloned.1.call-start = ((), (), s32[]{:S(2)}) async-start(), calls=%async_computation.6 | async-start | bytes 35651584 | tf_op jit(solution)/shard_map/all_gather | solution.py:86
  449.3 10.6 %copy-start.5 = (f32[2048,256]{1,0:T(8,128)S(1)}, f32[2048,256]{1,0:T(8,128)}, u32[]{:S(2)}) copy-start(f32[2048,256]{1,0:T(8,128)} %all-reduce.9.cloned.1.call-done) | copy-start | bytes 6291460
  459.9 4.8 copy-start.7
  461.2 3.4 copy-start.2
  669.5 13.5 %copy-start.1 = (f32[4096,128]{1,0:T(8,128)S(1)}, f32[4096,128]{1,0:T(8,128)}, u32[]{:S(2)}) copy-start(f32[4096,128]{1,0:T(8,128)} %param.14) | copy-start | bytes 6291460
Sparse Core Ops, SparseCore 0:
  120.3 62.1 all-reduce.6
  186.3 90.0 all-reduce.4
  293.0 62.3 all-reduce.10
  359.2 90.0 all-reduce.8
  473.1 196.3 all-gather.2
